TPU v7x, 256 devices: a whole 4x4x8 slice. The times are simulated.
256 devices in a mesh: wide: 32 (over x, z_hi, core), narrow: 8 (over y, z_lo).
Axes of the slice: x: 4, y: 4, z: 8 (z_hi: 4, z_lo: 2; z = z_hi * 2 + z_lo), core: 2. Of those that a mesh axis runs over, the one named last changes fastest.
Arguments:
- state_real: float32 [8, 32, 4096, 128], P('narrow', 'wide'), may hold values from -6 to 6
- state_imag: float32 [8, 32, 4096, 128], P('narrow', 'wide'), may hold values from -6 to 6
- gates: float32 [3, 2, 128, 128], replicated, may hold values from -0.375 to 0.375
- gate_orders: int32 [3, 7], replicated, may hold values from 0 to 6, each once within a row
- phase_masks: int32 [8, 2], replicated, may hold values from 1 to 67108864, as said below
- phase_angles: float32 [8], replicated, may hold values from -3.140625 to 3.140625
Outputs:
- out_real: float32 [8, 32, 4096, 128], P('narrow', 'wide')
- out_imag: float32 [8, 32, 4096, 128], P('narrow', 'wide')
Inputs may be any that keep to these rules, and one draw needn't show every extreme that they name: `phase_masks`: each entry is 2**q for one qubit q of the whole index of 134217728 amplitudes; the two entries of a row differ.
All inputs are finite; a program needn't handle non-finite values.
Results may differ from a plain program's by a relative error of at most 0.0003.
Values sent between devices are 32-bit elements; how exact they have to be, the bound alone decides.
No kernel may reach another device: no remote copies, remote signals or barrier semaphores. Data moves between devices by JAX's collectives and lax.ppermute only.
A program may use at most 64 MiB of HBM per device.

v0:
```python
import jax
import jax.numpy as jnp
from jax import lax
from jax.sharding import PartitionSpec as P

precise = lax.Precision.HIGHEST


def partner(block, axis, stride):
    count = lax.axis_size(axis)
    route = []
    for low in range(count):
        high = low | 1 << stride
        if high != low and high < count:
            route += [(low, high), (high, low)]
    return lax.ppermute(block, axis, route)


def ordered_gate(gate_pair, order_row):
    count = order_row.shape[0]
    states = jnp.arange(2**count, dtype=jnp.int32)
    places = jnp.arange(count, dtype=jnp.int32)
    digits = states[:, None] >> places[None, :] & 1
    mapped = jnp.sum(digits << order_row[None, :], axis=1)
    permute = (mapped[:, None] == states[None, :]).astype(jnp.float32)
    real_gate = jnp.dot(
        jnp.dot(permute, gate_pair[0], precision=precise), permute.T, precision=precise
    )
    imag_gate = jnp.dot(
        jnp.dot(permute, gate_pair[1], precision=precise), permute.T, precision=precise
    )
    return (real_gate, imag_gate)


def mixing(gate_real, gate_imag, real_part, imag_part):
    out_real = jnp.dot(gate_real, real_part, precision=precise) - jnp.dot(
        gate_imag, imag_part, precision=precise
    )
    out_imag = jnp.dot(gate_real, imag_part, precision=precise) + jnp.dot(
        gate_imag, real_part, precision=precise
    )
    return (out_real, out_imag)


def phase_turn(real_part, imag_part, flat, phase_masks, phase_angles):
    angle_sum = jnp.zeros(real_part.shape, jnp.float32)
    for which in range(phase_masks.shape[0]):
        both = (flat & phase_masks[which, 0] != 0) & (flat & phase_masks[which, 1] != 0)
        angle_sum = angle_sum + jnp.where(both, phase_angles[which], 0.0)
    cosine = jnp.cos(angle_sum)
    sine = jnp.sin(angle_sum)
    return (real_part * cosine - imag_part * sine, real_part * sine + imag_part * cosine)


def global_exchange(real_part, imag_part, gate_real, gate_imag, devices, outward, inward):
    row_count, columns = real_part.shape
    gate_size = gate_real.shape[0]
    blocks = gate_size // devices
    stride = row_count // blocks
    moved_real, moved_imag = outward(
        (
            real_part.reshape(1, blocks, stride, columns),
            imag_part.reshape(1, blocks, stride, columns),
        )
    )
    mixed_real, mixed_imag = mixing(
        gate_real, gate_imag, moved_real.reshape(gate_size, -1), moved_imag.reshape(gate_size, -1)
    )
    back_real, back_imag = inward(
        (mixed_real.reshape(moved_real.shape), mixed_imag.reshape(moved_imag.shape))
    )
    return (back_real.reshape(row_count, columns), back_imag.reshape(row_count, columns))


def swap_half(pieces, which_bit, own_index, sender):
    real_part, imag_part = pieces
    blocks, devices, stride, columns = real_part.shape
    split_shape = (blocks, devices >> which_bit + 1, 2, 1 << which_bit, stride, columns)
    own_bit = own_index >> which_bit & 1
    split_real = real_part.reshape(split_shape)
    split_imag = imag_part.reshape(split_shape)
    outgoing = (
        lax.dynamic_slice_in_dim(split_real, 1 - own_bit, 1, 2),
        lax.dynamic_slice_in_dim(split_imag, 1 - own_bit, 1, 2),
    )
    gotten = sender(outgoing, which_bit)
    result = []
    for kept_whole, arrived in ((split_real, gotten[0]), (split_imag, gotten[1])):
        kept_half = lax.dynamic_slice_in_dim(kept_whole, own_bit, 1, 2)
        joined = jnp.where(
            own_bit == 0,
            jnp.concatenate([kept_half, arrived], axis=2),
            jnp.concatenate([arrived, kept_half], axis=2),
        )
        result.append(joined.reshape(real_part.shape))
    return (result[0], result[1])


def global_halves(real_part, imag_part, gate_real, gate_imag, devices, own_index, sender):
    row_count, columns = real_part.shape
    gate_size = gate_real.shape[0]
    blocks = gate_size // devices
    stride = row_count // blocks
    local_shape = (blocks, devices, stride // devices, columns)
    pieces = (real_part.reshape(local_shape), imag_part.reshape(local_shape))
    levels = devices.bit_length() - 1
    for which_bit in range(levels):
        pieces = swap_half(pieces, which_bit, own_index, sender)
    turned_real = (
        gate_real.reshape(devices, blocks, devices, blocks)
        .transpose(1, 0, 3, 2)
        .reshape(gate_size, gate_size)
    )
    turned_imag = (
        gate_imag.reshape(devices, blocks, devices, blocks)
        .transpose(1, 0, 3, 2)
        .reshape(gate_size, gate_size)
    )
    mixed_real, mixed_imag = mixing(
        turned_real, turned_imag, pieces[0].reshape(gate_size, -1), pieces[1].reshape(gate_size, -1)
    )
    pieces = (mixed_real.reshape(local_shape), mixed_imag.reshape(local_shape))
    for which_bit in range(levels):
        pieces = swap_half(pieces, which_bit, own_index, sender)
    return (pieces[0].reshape(row_count, columns), pieces[1].reshape(row_count, columns))


def body(state_real, state_imag, gates, gate_orders, phase_masks, phase_angles):
    real_part = state_real[0, 0]
    imag_part = state_imag[0, 0]
    row_count, columns = real_part.shape
    first_gate = ordered_gate(gates[0], gate_orders[0])
    second_gate = ordered_gate(gates[1], gate_orders[1])
    third_gate = ordered_gate(gates[2], gate_orders[2])
    new_real = jnp.dot(real_part, first_gate[0].T, precision=precise) - jnp.dot(
        imag_part, first_gate[1].T, precision=precise
    )
    new_imag = jnp.dot(imag_part, first_gate[0].T, precision=precise) + jnp.dot(
        real_part, first_gate[1].T, precision=precise
    )
    wide_count = lax.axis_size("wide")
    narrow_count = lax.axis_size("narrow")
    wide_index = lax.axis_index("wide")
    narrow_index = lax.axis_index("narrow")
    offset = (narrow_index * wide_count + wide_index) * (row_count * columns)
    flat = (
        offset
        + jnp.arange(row_count, dtype=jnp.int32)[:, None] * columns
        + jnp.arange(columns, dtype=jnp.int32)[None, :]
    )
    turned_real, turned_imag = phase_turn(new_real, new_imag, flat, phase_masks, phase_angles)
    middle_real, middle_imag = global_exchange(
        turned_real,
        turned_imag,
        second_gate[0],
        second_gate[1],
        wide_count,
        lambda pieces: (
            lax.all_to_all(pieces[0], "wide", split_axis=2, concat_axis=0, tiled=True),
            lax.all_to_all(pieces[1], "wide", split_axis=2, concat_axis=0, tiled=True),
        ),
        lambda pieces: (
            lax.all_to_all(pieces[0], "wide", split_axis=0, concat_axis=2, tiled=True),
            lax.all_to_all(pieces[1], "wide", split_axis=0, concat_axis=2, tiled=True),
        ),
    )
    final_real, final_imag = global_halves(
        middle_real,
        middle_imag,
        third_gate[0],
        third_gate[1],
        narrow_count,
        narrow_index,
        lambda pieces, which_bit: partner((pieces[0], pieces[1]), "narrow", which_bit),
    )
    return (final_real[None, None], final_imag[None, None])


def solution(mesh):
    placed = (P("narrow", "wide", None, None), P("narrow", "wide", None, None), P(), P(), P(), P())
    return jax.shard_map(
        body,
        mesh=mesh,
        in_specs=placed,
        out_specs=(P("narrow", "wide", None, None), P("narrow", "wide", None, None)),
        check_vma=False,
    )
```

profile of v0, /device:TPU:2, one launch (start us, length us, event | category | flops | bytes accessed | tf_op | source)
XLA Modules:
  0.0 565.0 jit_solution(16842037079720946697)
XLA Ops:
  7.9 3.5 fusion.14
  15.4 30.1 %multiply_subtract_fusion = (f32[4096,128]{0,1:T(8,128)}, f32[4096,128]{0,1:T(8,128)S(1)}) fusion(f32[4096,128]{0,1:T(8,128)S(1)} %fusion.1, f32[]{:T(128)} %bitcast.34, s32[]{:T(128)} %bitcast.33, s32[]{:T(128)} %bitcast.32, f32[]{:T(128)} %bitcast.31, s32[]{:T(128)} %bitcast.30, s32[]{:T(128)} %bitcast.29, f32[]{:T(128)} %bitcast.28, s32[]{:T(128)} %bitcast.27, ...), kind=kOutput, calls=%fused_computation.39 | convolution fusion | flops 836763648 | bytes 10567776 | tf_op jit(solution)/shard_map/dot_general | solution.py:138
  45.5 26.3 %multiply_add_fusion = f32[4096,128]{0,1:T(8,128)S(1)} fusion(f32[4096,128]{0,1:T(8,128)S(1)} %get-tuple-element.54, f32[4096,128]{0,1:T(8,128)S(1)} %fusion.1, f32[]{:T(128)} %bitcast.34, s32[]{:T(128)} %bitcast.33, s32[]{:T(128)} %bitcast.32, f32[]{:T(128)} %bitcast.31, s32[]{:T(128)} %bitcast.30, s32[]{:T(128)} %bitcast.29, f32[]{:T(128)} %bitcast.28, ...), kind=kLoop, calls=%fused_computation.38 | loop fusion | flops 30932992 | bytes 6307936 | tf_op jit(solution)/shard_map/add | solution.py:52
  74.3 3.9 copy.46
  78.2 11.6 %all-to-all-start.1 = ((f32[1,4,1024,128]{3,1,0,2:T(4,128)}), f32[1,4,1024,128]{3,1,0,2:T(4,128)S(1)}, u32[]{:S(2)}, u32[]{:S(2)}) async-start(f32[1,4,1024,128]{3,1,0,2:T(4,128)} %copy.46), calls=%async_computation.1 | async-start | bytes 4194304 | tf_op jit(solution)/shard_map/all_to_all | solution.py:160
  89.8 3.6 reshape.422
  93.5 3.9 copy.43
  97.4 39.9 %all-to-all-done.1 = f32[1,4,1024,128]{3,1,0,2:T(4,128)S(1)} async-done(((f32[1,4,1024,128]{3,1,0,2:T(4,128)}), f32[1,4,1024,128]{3,1,0,2:T(4,128)S(1)}, u32[]{:S(2)}, u32[]{:S(2)}) %all-to-all-start.1) | async-done | bytes 2097184 | tf_op jit(solution)/shard_map/all_to_all | solution.py:160
  137.2 8.6 %all-to-all-start = ((f32[1,4,1024,128]{3,1,0,2:T(4,128)}), f32[1,4,1024,128]{3,1,0,2:T(4,128)}, u32[]{:S(2)}, u32[]{:S(2)}) async-start(f32[1,4,1024,128]{3,1,0,2:T(4,128)} %copy.43), calls=%async_computation | async-start | bytes 4194304 | tf_op jit(solution)/shard_map/all_to_all | solution.py:159
  147.3 39.6 %all-to-all-done = f32[1,4,1024,128]{3,1,0,2:T(4,128)} async-done(((f32[1,4,1024,128]{3,1,0,2:T(4,128)}), f32[1,4,1024,128]{3,1,0,2:T(4,128)}, u32[]{:S(2)}, u32[]{:S(2)}) %all-to-all-start) | async-done | bytes 2097184 | tf_op jit(solution)/shard_map/all_to_all | solution.py:159
  191.9 3.0 fusion.36
  196.7 15.0 %all-to-all-start.2 = ((f32[32,4,32,128]{3,2,1,0:T(8,128)}), f32[32,4,32,128]{3,2,1,0:T(8,128)}, u32[]{:S(2)}, u32[]{:S(2)}) async-start(f32[32,4,32,128]{3,2,1,0:T(8,128)} %bitcast.200), calls=%async_computation.2 | async-start | bytes 4194304 | tf_op jit(solution)/shard_map/all_to_all | solution.py:163
  214.7 3.1 fusion.39
  219.5 34.7 %all-to-all-done.2 = f32[32,4,32,128]{3,2,1,0:T(8,128)} async-done(((f32[32,4,32,128]{3,2,1,0:T(8,128)}), f32[32,4,32,128]{3,2,1,0:T(8,128)}, u32[]{:S(2)}, u32[]{:S(2)}) %all-to-all-start.2) | async-done | bytes 2097184 | tf_op jit(solution)/shard_map/all_to_all | solution.py:163
  254.2 13.6 %all-to-all-start.3 = ((f32[32,4,32,128]{3,2,1,0:T(8,128)}), f32[32,4,32,128]{3,2,1,0:T(8,128)}, u32[]{:S(2)}, u32[]{:S(2)}) async-start(f32[32,4,32,128]{3,2,1,0:T(8,128)} %bitcast.199), calls=%async_computation.3 | async-start | bytes 4194304 | tf_op jit(solution)/shard_map/all_to_all | solution.py:164
  273.7 36.9 %all-to-all-done.3 = f32[32,4,32,128]{3,2,1,0:T(8,128)} async-done(((f32[32,4,32,128]{3,2,1,0:T(8,128)}), f32[32,4,32,128]{3,2,1,0:T(8,128)}, u32[]{:S(2)}, u32[]{:S(2)}) %all-to-all-start.3) | async-done | bytes 2097184 | tf_op jit(solution)/shard_map/all_to_all | solution.py:164
  313.7 8.5 %collective-permute-start.3 = (f32[16,4,1,1,32,128]{5,4,2,1,0,3:T(8,128)}, f32[16,4,1,1,32,128]{5,4,2,1,0,3:T(8,128)}, u32[]{:S(2)}, u32[]{:S(2)}) collective-permute-start(f32[16,4,1,1,32,128]{5,4,2,1,0,3:T(8,128)} %get-tuple-element.19), channel_id=1, source_target_pairs={{0,1},{1,0},{2,3},{3,2},{4,5},{5,4},{6,7},{7,6},{8,9},{9,8},{10,11... | collective-permute-start | bytes 3145736 | tf_op jit(solution)/shard_map/ppermute | solution.py:16
  322.2 16.6 %collective-permute-done = f32[16,4,1,1,32,128]{5,4,2,1,0,3:T(8,128)} collective-permute-done((f32[16,4,1,1,32,128]{5,4,2,1,0,3:T(8,128)}, f32[16,4,1,1,32,128]{5,4,2,1,0,3:T(8,128)}, u32[]{:S(2)}, u32[]{:S(2)}) %collective-permute-start) | collective-permute-done | bytes 1048608 | tf_op jit(solution)/shard_map/ppermute | solution.py:16
  345.7 15.5 %collective-permute-done.3 = f32[16,4,1,1,32,128]{5,4,2,1,0,3:T(8,128)} collective-permute-done((f32[16,4,1,1,32,128]{5,4,2,1,0,3:T(8,128)}, f32[16,4,1,1,32,128]{5,4,2,1,0,3:T(8,128)}, u32[]{:S(2)}, u32[]{:S(2)}) %collective-permute-start.3) | collective-permute-done | bytes 1048608 | tf_op jit(solution)/shard_map/ppermute | solution.py:16
  366.4 3.6 collective-permute-done.1
  369.9 3.0 maximum_select_fusion.1
  376.7 15.7 %collective-permute-done.4 = f32[16,2,1,2,32,128]{5,4,3,2,1,0:T(8,128)} collective-permute-done((f32[16,2,1,2,32,128]{5,4,3,2,1,0:T(8,128)}, f32[16,2,1,2,32,128]{5,4,3,2,1,0:T(8,128)}, u32[]{:S(2)}, u32[]{:S(2)}) %collective-permute-start.4) | collective-permute-done | bytes 1048608 | tf_op jit(solution)/shard_map/ppermute | solution.py:16
  400.5 15.2 %collective-permute-done.2 = f32[16,1,1,4,32,128]{5,4,3,2,0,1:T(8,128)} collective-permute-done((f32[16,1,1,4,32,128]{5,4,3,2,0,1:T(8,128)}, f32[16,1,1,4,32,128]{5,4,3,2,0,1:T(8,128)}, u32[]{:S(2)}, u32[]{:S(2)}) %collective-permute-start.2) | collective-permute-done | bytes 1048608 | tf_op jit(solution)/shard_map/ppermute | solution.py:16
  417.8 3.0 fusion.6
  420.8 16.4 %collective-permute-done.5 = f32[16,1,1,4,32,128]{5,4,3,2,0,1:T(8,128)} collective-permute-done((f32[16,1,1,4,32,128]{5,4,3,2,0,1:T(8,128)}, f32[16,1,1,4,32,128]{5,4,3,2,0,1:T(8,128)}, u32[]{:S(2)}, u32[]{:S(2)}) %collective-permute-start.5) | collective-permute-done | bytes 1048608 | tf_op jit(solution)/shard_map/ppermute | solution.py:16
  442.1 3.0 fusion.42
  446.3 3.0 fusion.45
  451.7 20.3 %collective-permute-done.6 = f32[16,4,1,1,32,128]{5,4,2,1,0,3:T(8,128)S(1)} collective-permute-done((f32[16,4,1,1,32,128]{5,4,2,1,0,3:T(8,128)S(1)}, f32[16,4,1,1,32,128]{5,4,2,1,0,3:T(8,128)S(1)}, u32[]{:S(2)}, u32[]{:S(2)}) %collective-permute-start.6) | collective-permute-done | bytes 1048608 | tf_op jit(solution)/shard_map/ppermute | solution.py:16
  472.7 20.0 %collective-permute-done.9 = f32[16,4,1,1,32,128]{5,4,2,1,0,3:T(8,128)S(1)} collective-permute-done((f32[16,4,1,1,32,128]{5,4,2,1,0,3:T(8,128)S(1)}, f32[16,4,1,1,32,128]{5,4,2,1,0,3:T(8,128)S(1)}, u32[]{:S(2)}, u32[]{:S(2)}) %collective-permute-start.9) | collective-permute-done | bytes 1048608 | tf_op jit(solution)/shard_map/ppermute | solution.py:16
  496.8 22.5 %collective-permute-done.10 = f32[16,2,1,2,32,128]{5,4,3,2,1,0:T(8,128)S(1)} collective-permute-done((f32[16,2,1,2,32,128]{5,4,3,2,1,0:T(8,128)S(1)}, f32[16,2,1,2,32,128]{5,4,3,2,1,0:T(8,128)S(1)}, u32[]{:S(2)}, u32[]{:S(2)}) %collective-permute-start.10) | collective-permute-done | bytes 1048608 | tf_op jit(solution)/shard_map/ppermute | solution.py:16
  521.9 20.8 %collective-permute-done.8 = f32[16,1,1,4,32,128]{5,4,3,2,0,1:T(8,128)S(1)} collective-permute-done((f32[16,1,1,4,32,128]{5,4,3,2,0,1:T(8,128)S(1)}, f32[16,1,1,4,32,128]{5,4,3,2,0,1:T(8,128)S(1)}, u32[]{:S(2)}, u32[]{:S(2)}) %collective-permute-start.8) | collective-permute-done | bytes 1048608 | tf_op jit(solution)/shard_map/ppermute | solution.py:16
  544.3 18.1 %collective-permute-done.11 = f32[16,1,1,4,32,128]{5,4,3,2,0,1:T(8,128)S(1)} collective-permute-done((f32[16,1,1,4,32,128]{5,4,3,2,0,1:T(8,128)S(1)}, f32[16,1,1,4,32,128]{5,4,3,2,0,1:T(8,128)S(1)}, u32[]{:S(2)}, u32[]{:S(2)}) %collective-permute-start.11) | collective-permute-done | bytes 1048608 | tf_op jit(solution)/shard_map/ppermute | solution.py:16
  (91 shorter events, 80.8 us)
Async XLA Ops:
  0.6 10.8 %copy-start = (f32[1,1,4096,128]{3,2,1,0:T(8,128)S(1)}, f32[1,1,4096,128]{3,2,1,0:T(8,128)}, u32[]{:S(2)}) copy-start(f32[1,1,4096,128]{3,2,1,0:T(8,128)} %param.6) | copy-start | bytes 6291460
  11.4 2.0 copy-start.4
  78.2 59.0 %all-to-all-start.1 = ((f32[1,4,1024,128]{3,1,0,2:T(4,128)}), f32[1,4,1024,128]{3,1,0,2:T(4,128)S(1)}, u32[]{:S(2)}, u32[]{:S(2)}) async-start(f32[1,4,1024,128]{3,1,0,2:T(4,128)} %copy.46), calls=%async_computation.1 | async-start | bytes 4194304 | tf_op jit(solution)/shard_map/all_to_all | solution.py:160
  97.4 48.5 %copy-start.7 = (f32[3,2,128,128]{3,2,1,0:T(8,128)S(1)}, f32[3,2,128,128]{3,2,1,0:T(8,128)}, u32[]{:S(2)}) copy-start(f32[3,2,128,128]{3,2,1,0:T(8,128)} %param.8) | copy-start | bytes 1179652
  137.2 49.7 %all-to-all-start = ((f32[1,4,1024,128]{3,1,0,2:T(4,128)}), f32[1,4,1024,128]{3,1,0,2:T(4,128)}, u32[]{:S(2)}, u32[]{:S(2)}) async-start(f32[1,4,1024,128]{3,1,0,2:T(4,128)} %copy.43), calls=%async_computation | async-start | bytes 4194304 | tf_op jit(solution)/shard_map/all_to_all | solution.py:159
  188.9 3.0 copy-start.2
  196.7 57.5 %all-to-all-start.2 = ((f32[32,4,32,128]{3,2,1,0:T(8,128)}), f32[32,4,32,128]{3,2,1,0:T(8,128)}, u32[]{:S(2)}, u32[]{:S(2)}) async-start(f32[32,4,32,128]{3,2,1,0:T(8,128)} %bitcast.200), calls=%async_computation.2 | async-start | bytes 4194304 | tf_op jit(solution)/shard_map/all_to_all | solution.py:163
  211.6 3.0 copy-start.3
  254.2 56.5 %all-to-all-start.3 = ((f32[32,4,32,128]{3,2,1,0:T(8,128)}), f32[32,4,32,128]{3,2,1,0:T(8,128)}, u32[]{:S(2)}, u32[]{:S(2)}) async-start(f32[32,4,32,128]{3,2,1,0:T(8,128)} %bitcast.199), calls=%async_computation.3 | async-start | bytes 4194304 | tf_op jit(solution)/shard_map/all_to_all | solution.py:164
  271.2 67.6 %collective-permute-start = (f32[16,4,1,1,32,128]{5,4,2,1,0,3:T(8,128)}, f32[16,4,1,1,32,128]{5,4,2,1,0,3:T(8,128)}, u32[]{:S(2)}, u32[]{:S(2)}) collective-permute-start(f32[16,4,1,1,32,128]{5,4,2,1,0,3:T(8,128)} %get-tuple-element.25), channel_id=1, source_target_pairs={{0,1},{1,0},{2,3},{3,2},{4,5},{5,4},{6,7},{7,6},{8,9},{9,8},{10,11... | collective-permute-start | bytes 3145736 | tf_op jit(solution)/shard_map/ppermute | solution.py:16
  313.7 47.5 %collective-permute-start.3 = (f32[16,4,1,1,32,128]{5,4,2,1,0,3:T(8,128)}, f32[16,4,1,1,32,128]{5,4,2,1,0,3:T(8,128)}, u32[]{:S(2)}, u32[]{:S(2)}) collective-permute-start(f32[16,4,1,1,32,128]{5,4,2,1,0,3:T(8,128)} %get-tuple-element.19), channel_id=1, source_target_pairs={{0,1},{1,0},{2,3},{3,2},{4,5},{5,4},{6,7},{7,6},{8,9},{9,8},{10,11... | collective-permute-start | bytes 3145736 | tf_op jit(solution)/shard_map/ppermute | solution.py:16
  343.2 26.7 %collective-permute-start.1 = (f32[16,2,1,2,32,128]{5,4,3,2,1,0:T(8,128)}, f32[16,2,1,2,32,128]{5,4,3,2,1,0:T(8,128)}, u32[]{:S(2)}, u32[]{:S(2)}) collective-permute-start(f32[16,2,1,2,32,128]{5,4,3,2,1,0:T(8,128)} %get-tuple-element.23), channel_id=1, source_target_pairs={{0,2},{2,0},{1,3},{3,1},{4,6},{6,4},{5,7},{7,5},{8,10},{10,8},{9,1... | collective-permute-start | bytes 3145736 | tf_op jit(solution)/shard_map/ppermute | solution.py:16
  364.3 28.1 %collective-permute-start.4 = (f32[16,2,1,2,32,128]{5,4,3,2,1,0:T(8,128)}, f32[16,2,1,2,32,128]{5,4,3,2,1,0:T(8,128)}, u32[]{:S(2)}, u32[]{:S(2)}) collective-permute-start(f32[16,2,1,2,32,128]{5,4,3,2,1,0:T(8,128)} %get-tuple-element.17), channel_id=1, source_target_pairs={{0,2},{2,0},{1,3},{3,1},{4,6},{6,4},{5,7},{7,5},{8,10},{10,8},{9,1... | collective-permute-start | bytes 3145736 | tf_op jit(solution)/shard_map/ppermute | solution.py:16
  374.6 41.1 %collective-permute-start.2 = (f32[16,1,1,4,32,128]{5,4,3,2,0,1:T(8,128)}, f32[16,1,1,4,32,128]{5,4,3,2,0,1:T(8,128)}, u32[]{:S(2)}, u32[]{:S(2)}) collective-permute-start(f32[16,1,1,4,32,128]{5,4,3,2,0,1:T(8,128)} %get-tuple-element.21), channel_id=1, source_target_pairs={{0,4},{4,0},{1,5},{5,1},{2,6},{6,2},{3,7},{7,3},{8,12},{12,8},{9,1... | collective-permute-start | bytes 3145736 | tf_op jit(solution)/shard_map/ppermute | solution.py:16
  396.0 41.2 %collective-permute-start.5 = (f32[16,1,1,4,32,128]{5,4,3,2,0,1:T(8,128)}, f32[16,1,1,4,32,128]{5,4,3,2,0,1:T(8,128)}, u32[]{:S(2)}, u32[]{:S(2)}) collective-permute-start(f32[16,1,1,4,32,128]{5,4,3,2,0,1:T(8,128)} %get-tuple-element.15), channel_id=1, source_target_pairs={{0,4},{4,0},{1,5},{5,1},{2,6},{6,2},{3,7},{7,3},{8,12},{12,8},{9,1... | collective-permute-start | bytes 3145736 | tf_op jit(solution)/shard_map/ppermute | solution.py:16
  399.1 16.6 %copy-start.5 = (f32[16,1,1,4,32,128]{5,4,3,2,0,1:T(8,128)S(1)}, f32[16,1,1,4,32,128]{5,4,3,2,0,1:T(8,128)}, u32[]{:S(2)}) copy-start(f32[16,1,1,4,32,128]{5,4,3,2,0,1:T(8,128)} %get-tuple-element.20) | copy-start | bytes 3145732
  417.8 19.5 %copy-start.6 = (f32[16,1,1,4,32,128]{5,4,3,2,0,1:T(8,128)S(1)}, f32[16,1,1,4,32,128]{5,4,3,2,0,1:T(8,128)}, u32[]{:S(2)}) copy-start(f32[16,1,1,4,32,128]{5,4,3,2,0,1:T(8,128)} %get-tuple-element.14) | copy-start | bytes 3145732
  445.9 26.1 %collective-permute-start.6 = (f32[16,4,1,1,32,128]{5,4,2,1,0,3:T(8,128)S(1)}, f32[16,4,1,1,32,128]{5,4,2,1,0,3:T(8,128)S(1)}, u32[]{:S(2)}, u32[]{:S(2)}) collective-permute-start(f32[16,4,1,1,32,128]{5,4,2,1,0,3:T(8,128)S(1)} %get-tuple-element.13), channel_id=1, source_target_pairs={{0,1},{1,0},{2,3},{3,2},{4,5},{5,4},{6,7},{7,6},{8,9},{9,8},{10,11... | collective-permute-start | bytes 3145736 | tf_op jit(solution)/shard_map/ppermute | solution.py:16
  449.9 42.8 %collective-permute-start.9 = (f32[16,4,1,1,32,128]{5,4,2,1,0,3:T(8,128)S(1)}, f32[16,4,1,1,32,128]{5,4,2,1,0,3:T(8,128)S(1)}, u32[]{:S(2)}, u32[]{:S(2)}) collective-permute-start(f32[16,4,1,1,32,128]{5,4,2,1,0,3:T(8,128)S(1)} %get-tuple-element.7), channel_id=1, source_target_pairs={{0,1},{1,0},{2,3},{3,2},{4,5},{5,4},{6,7},{7,6},{8,9},{9,8},{10,11... | collective-permute-start | bytes 3145736 | tf_op jit(solution)/shard_map/ppermute | solution.py:16
  472.5 21.7 %collective-permute-start.7 = (f32[16,2,1,2,32,128]{5,4,3,2,1,0:T(8,128)S(1)}, f32[16,2,1,2,32,128]{5,4,3,2,1,0:T(8,128)S(1)}, u32[]{:S(2)}, u32[]{:S(2)}) collective-permute-start(f32[16,2,1,2,32,128]{5,4,3,2,1,0:T(8,128)S(1)} %get-tuple-element.11), channel_id=1, source_target_pairs={{0,2},{2,0},{1,3},{3,1},{4,6},{6,4},{5,7},{7,5},{8,10},{10,8},{9,1... | collective-permute-start | bytes 3145736 | tf_op jit(solution)/shard_map/ppermute | solution.py:16
  493.1 26.1 %collective-permute-start.10 = (f32[16,2,1,2,32,128]{5,4,3,2,1,0:T(8,128)S(1)}, f32[16,2,1,2,32,128]{5,4,3,2,1,0:T(8,128)S(1)}, u32[]{:S(2)}, u32[]{:S(2)}) collective-permute-start(f32[16,2,1,2,32,128]{5,4,3,2,1,0:T(8,128)S(1)} %get-tuple-element.5), channel_id=1, source_target_pairs={{0,2},{2,0},{1,3},{3,1},{4,6},{6,4},{5,7},{7,5},{8,10},{10,8},{9,1... | collective-permute-start | bytes 3145736 | tf_op jit(solution)/shard_map/ppermute | solution.py:16
  494.6 48.2 %collective-permute-start.8 = (f32[16,1,1,4,32,128]{5,4,3,2,0,1:T(8,128)S(1)}, f32[16,1,1,4,32,128]{5,4,3,2,0,1:T(8,128)S(1)}, u32[]{:S(2)}, u32[]{:S(2)}) collective-permute-start(f32[16,1,1,4,32,128]{5,4,3,2,0,1:T(8,128)S(1)} %get-tuple-element.9), channel_id=1, source_target_pairs={{0,4},{4,0},{1,5},{5,1},{2,6},{6,2},{3,7},{7,3},{8,12},{12,8},{9,1... | collective-permute-start | bytes 3145736 | tf_op jit(solution)/shard_map/ppermute | solution.py:16
  519.7 42.7 %collective-permute-start.11 = (f32[16,1,1,4,32,128]{5,4,3,2,0,1:T(8,128)S(1)}, f32[16,1,1,4,32,128]{5,4,3,2,0,1:T(8,128)S(1)}, u32[]{:S(2)}, u32[]{:S(2)}) collective-permute-start(f32[16,1,1,4,32,128]{5,4,3,2,0,1:T(8,128)S(1)} %get-tuple-element.3), channel_id=1, source_target_pairs={{0,4},{4,0},{1,5},{5,1},{2,6},{6,2},{3,7},{7,3},{8,12},{12,8},{9,1... | collective-permute-start | bytes 3145736 | tf_op jit(solution)/shard_map/ppermute | solution.py:16
  562.4 2.3 copy-start.1
where the time goes:
time: 575 us; the launch traced here: 565 us
  waiting for transfers between devices  337 us (59%)
  starting transfers between devices  75 us (13%)
  matrix products  66.5 us (12%)
  other arithmetic  44.2 us (8%)
  local copies, waits for them, and re-layouts  41.4 us (7%)
    ppermute x12, waiting for transfers between devices, partner(): return lax.ppermute(block, axis, route)  185 us
    all_to_all x1, waiting for transfers between devices, body(): lax.all_to_all(pieces[1], 'wide', split_axis=2, concat_axis=0, tiled=True)  39.9 us
    all_to_all x1, waiting for transfers between devices, body(): lax.all_to_all(pieces[0], 'wide', split_axis=2, concat_axis=0, tiled=True)  39.6 us
    all_to_all x1, waiting for transfers between devices, body(): lax.all_to_all(pieces[1], 'wide', split_axis=0, concat_axis=2, tiled=True)  36.9 us
    all_to_all x1, waiting for transfers between devices, body(): lax.all_to_all(pieces[0], 'wide', split_axis=0, concat_axis=2, tiled=True)  34.7 us
    dot_general x1, matrix products, body(): jnp.dot(real_part, first_gate[1].T, precision=precise)  30.1 us
    add x1, other arithmetic, phase_turn(): real_part * sine + imag_part * cosine  26.3 us
    ppermute x12, starting transfers between devices, partner(): return lax.ppermute(block, axis, route)  26.2 us
  transfers between devices with their start and end apart: 16, of which 16 were waited for; matrix products, arithmetic and copies ran while one was open for 10% of the time, Pallas kernels for 0%

commit v1 on v0

--- a/solution.py
+++ b/solution.py
@@ -157,7 +157,12 @@
         wide_count,
         lambda pieces: (
             lax.all_to_all(pieces[0], "wide", split_axis=2, concat_axis=0, tiled=True),
-            lax.all_to_all(pieces[1], "wide", split_axis=2, concat_axis=0, tiled=True),
+            jnp.concatenate(
+                lax.all_to_all(
+                    jnp.stack(jnp.split(pieces[1], lax.axis_size("wide"), axis=2)), "wide", 0, 0
+                ),
+                axis=0,
+            ),
         ),
         lambda pieces: (
             lax.all_to_all(pieces[0], "wide", split_axis=0, concat_axis=2, tiled=True),

time: 575 us -> 550 us (0.957)
  waiting for transfers between devices: 337 us -> 302 us
  local copies, waits for them, and re-layouts: 41.4 us -> 53.7 us
  starting transfers between devices: 75 us -> 64.5 us
  matrix products: 66.5 us -> 72.3 us
    all_to_all x1, waiting for transfers between devices: 39.6 us -> 0.01 us  [body(): lax.all_to_all(pieces[0], 'wide', split_axis=2, concat_axis=0, tiled=True)]
    unnamed x20 -> x59, local copies, waits for them, and re-layouts: 5.12 us -> 24.8 us
  transfers between devices with their start and end apart: 16 -> 16, of which waited for: 16 -> 15; matrix products, arithmetic and copies ran while one was open for 10% -> 19% of each run, Pallas kernels for 0% -> 0%
where the time goes in v1:
time: 550 us; the launch traced here: 540 us
  waiting for transfers between devices  302 us (55%)
  matrix products  72.3 us (13%)
  starting transfers between devices  64.5 us (12%)
  local copies, waits for them, and re-layouts  53.7 us (10%)
  other arithmetic  46 us (8%)
    ppermute x12, waiting for transfers between devices, partner(): return lax.ppermute(block, axis, route)  186 us
    all_to_all x1, waiting for transfers between devices, body(): lax.all_to_all(jnp.stack(jnp.split(pieces[1], lax.axis_size('wide'), axis...  43.5 us
    all_to_all x1, waiting for transfers between devices, body(): lax.all_to_all(pieces[0], 'wide', split_axis=0, concat_axis=2, tiled=True)  39.8 us
    all_to_all x1, waiting for transfers between devices, body(): lax.all_to_all(pieces[1], 'wide', split_axis=0, concat_axis=2, tiled=True)  33.5 us
    dot_general x1, matrix products, body(): jnp.dot(real_part, first_gate[1].T, precision=precise)  30.2 us
    add x1, other arithmetic, phase_turn(): real_part * sine + imag_part * cosine  28.4 us
    unnamed x59, local copies, waits for them, and re-layouts  24.8 us
    ppermute x12, starting transfers between devices, partner(): return lax.ppermute(block, axis, route)  22.7 us
  transfers between devices with their start and end apart: 16, of which 15 were waited for; matrix products, arithmetic and copies ran while one was open for 19% of the time, Pallas kernels for 0%

profile of v1, /device:TPU:2, one launch (start us, length us, event | category | flops | bytes accessed | tf_op | source)
XLA Modules:
  0.0 540.1 jit_solution(10141467080731996586)
XLA Ops:
  4.4 3.3 fusion.18
  7.6 3.3 fusion.14
  12.3 4.3 fusion.1
  16.6 30.2 %multiply_subtract_fusion = (f32[4096,128]{0,1:T(8,128)}, f32[4096,128]{0,1:T(8,128)}) fusion(f32[4096,128]{0,1:T(8,128)S(1)} %fusion.1, f32[]{:T(128)} %bitcast.34, s32[]{:T(128)} %bitcast.33, s32[]{:T(128)} %bitcast.32, f32[]{:T(128)} %bitcast.31, s32[]{:T(128)} %bitcast.30, s32[]{:T(128)} %bitcast.29, f32[]{:T(128)} %bitcast.28, s32[]{:T(128)} %bitcast.27, ...), kind=kOutput, calls=%fused_computation.39 | convolution fusion | flops 836763648 | bytes 10567776 | tf_op jit(solution)/shard_map/dot_general | solution.py:138
  52.1 11.8 %all-to-all-start = ((f32[1,4,1024,128]{3,1,0,2:T(4,128)}), f32[1,4,1024,128]{3,1,0,2:T(4,128)}, u32[]{:S(2)}, u32[]{:S(2)}) async-start(f32[1,4,1024,128]{3,1,0,2:T(4,128)} %copy.132), calls=%async_computation | async-start | bytes 4194304 | tf_op jit(solution)/shard_map/all_to_all | solution.py:159
  63.9 28.4 %multiply_add_fusion = f32[4096,128]{0,1:T(8,128)} fusion(f32[4096,128]{0,1:T(8,128)} %get-tuple-element.54, f32[4096,128]{0,1:T(8,128)S(1)} %copy-done.5, f32[]{:T(128)} %bitcast.34, s32[]{:T(128)} %bitcast.33, s32[]{:T(128)} %bitcast.32, f32[]{:T(128)} %bitcast.31, s32[]{:T(128)} %bitcast.30, s32[]{:T(128)} %bitcast.29, f32[]{:T(128)} %bitcast.28, ...), kind=kLoop, calls=%fused_computation.38 | loop fusion | flops 30932992 | bytes 6307936 | tf_op jit(solution)/shard_map/add | solution.py:52
  114.5 10.2 %all-to-all-start.1 = ((f32[32,1,4,32,128]{4,3,2,1,0:T(8,128)}), f32[32,1,4,32,128]{4,3,2,1,0:T(8,128)S(1)}, u32[]{:S(2)}, u32[]{:S(2)}) async-start(f32[32,1,4,32,128]{4,3,2,1,0:T(8,128)} %constant_dynamic-update-slice_fusion), calls=%async_computation.1 | async-start | bytes 4194304 | tf_op jit(solution)/shard_map/all_to_all | solution.py:161
  129.1 43.5 %all-to-all-done.1 = f32[32,1,4,32,128]{4,3,2,1,0:T(8,128)S(1)} async-done(((f32[32,1,4,32,128]{4,3,2,1,0:T(8,128)}), f32[32,1,4,32,128]{4,3,2,1,0:T(8,128)S(1)}, u32[]{:S(2)}, u32[]{:S(2)}) %all-to-all-start.1) | async-done | bytes 2097184 | tf_op jit(solution)/shard_map/all_to_all | solution.py:161
  175.6 3.0 fusion.39
  180.4 9.0 %all-to-all-start.3 = ((f32[32,4,32,128]{3,2,1,0:T(8,128)}), f32[32,4,32,128]{3,2,1,0:T(8,128)}, u32[]{:S(2)}, u32[]{:S(2)}) async-start(f32[32,4,32,128]{3,2,1,0:T(8,128)} %bitcast.354), calls=%async_computation.3 | async-start | bytes 4194304 | tf_op jit(solution)/shard_map/all_to_all | solution.py:169
  189.3 4.6 fusion.12
  193.9 3.0 fusion.36
  198.6 33.5 %all-to-all-done.3 = f32[32,4,32,128]{3,2,1,0:T(8,128)} async-done(((f32[32,4,32,128]{3,2,1,0:T(8,128)}), f32[32,4,32,128]{3,2,1,0:T(8,128)}, u32[]{:S(2)}, u32[]{:S(2)}) %all-to-all-start.3) | async-done | bytes 2097184 | tf_op jit(solution)/shard_map/all_to_all | solution.py:169
  232.1 10.8 %all-to-all-start.2 = ((f32[32,4,32,128]{3,2,1,0:T(8,128)}), f32[32,4,32,128]{3,2,1,0:T(8,128)}, u32[]{:S(2)}, u32[]{:S(2)}) async-start(f32[32,4,32,128]{3,2,1,0:T(8,128)} %bitcast.113), calls=%async_computation.2 | async-start | bytes 4194304 | tf_op jit(solution)/shard_map/all_to_all | solution.py:168
  246.3 4.3 collective-permute-start.3
  250.6 39.8 %all-to-all-done.2 = f32[32,4,32,128]{3,2,1,0:T(8,128)} async-done(((f32[32,4,32,128]{3,2,1,0:T(8,128)}), f32[32,4,32,128]{3,2,1,0:T(8,128)}, u32[]{:S(2)}, u32[]{:S(2)}) %all-to-all-start.2) | async-done | bytes 2097184 | tf_op jit(solution)/shard_map/all_to_all | solution.py:168
  293.4 4.2 collective-permute-start
  297.6 16.2 %collective-permute-done.3 = f32[16,4,1,1,32,128]{5,4,2,1,0,3:T(8,128)} collective-permute-done((f32[16,4,1,1,32,128]{5,4,2,1,0,3:T(8,128)}, f32[16,4,1,1,32,128]{5,4,2,1,0,3:T(8,128)}, u32[]{:S(2)}, u32[]{:S(2)}) %collective-permute-start.3) | collective-permute-done | bytes 1048608 | tf_op jit(solution)/shard_map/ppermute | solution.py:16
  319.9 16.4 %collective-permute-done = f32[16,4,1,1,32,128]{5,4,2,1,0,3:T(8,128)} collective-permute-done((f32[16,4,1,1,32,128]{5,4,2,1,0,3:T(8,128)}, f32[16,4,1,1,32,128]{5,4,2,1,0,3:T(8,128)}, u32[]{:S(2)}, u32[]{:S(2)}) %collective-permute-start) | collective-permute-done | bytes 1048608 | tf_op jit(solution)/shard_map/ppermute | solution.py:16
  341.0 3.7 collective-permute-done.4
  349.1 3.6 collective-permute-start.5
  352.9 14.2 %collective-permute-done.1 = f32[16,2,1,2,32,128]{5,4,3,2,1,0:T(8,128)} collective-permute-done((f32[16,2,1,2,32,128]{5,4,3,2,1,0:T(8,128)}, f32[16,2,1,2,32,128]{5,4,3,2,1,0:T(8,128)}, u32[]{:S(2)}, u32[]{:S(2)}) %collective-permute-start.1) | collective-permute-done | bytes 1048608 | tf_op jit(solution)/shard_map/ppermute | solution.py:16
  370.7 3.2 collective-permute-start.2
  377.7 14.3 %collective-permute-done.5 = f32[16,1,1,4,32,128]{5,4,3,2,0,1:T(8,128)} collective-permute-done((f32[16,1,1,4,32,128]{5,4,3,2,0,1:T(8,128)}, f32[16,1,1,4,32,128]{5,4,3,2,0,1:T(8,128)}, u32[]{:S(2)}, u32[]{:S(2)}) %collective-permute-start.5) | collective-permute-done | bytes 1048608 | tf_op jit(solution)/shard_map/ppermute | solution.py:16
  397.0 16.5 %collective-permute-done.2 = f32[16,1,1,4,32,128]{5,4,3,2,0,1:T(8,128)} collective-permute-done((f32[16,1,1,4,32,128]{5,4,3,2,0,1:T(8,128)}, f32[16,1,1,4,32,128]{5,4,3,2,0,1:T(8,128)}, u32[]{:S(2)}, u32[]{:S(2)}) %collective-permute-start.2) | collective-permute-done | bytes 1048608 | tf_op jit(solution)/shard_map/ppermute | solution.py:16
  418.5 3.0 fusion.45
  422.4 3.0 fusion.42
  428.1 20.3 %collective-permute-done.9 = f32[16,4,1,1,32,128]{5,4,2,1,0,3:T(8,128)S(1)} collective-permute-done((f32[16,4,1,1,32,128]{5,4,2,1,0,3:T(8,128)S(1)}, f32[16,4,1,1,32,128]{5,4,2,1,0,3:T(8,128)S(1)}, u32[]{:S(2)}, u32[]{:S(2)}) %collective-permute-start.9) | collective-permute-done | bytes 1048608 | tf_op jit(solution)/shard_map/ppermute | solution.py:16
  449.1 20.0 %collective-permute-done.6 = f32[16,4,1,1,32,128]{5,4,2,1,0,3:T(8,128)S(1)} collective-permute-done((f32[16,4,1,1,32,128]{5,4,2,1,0,3:T(8,128)S(1)}, f32[16,4,1,1,32,128]{5,4,2,1,0,3:T(8,128)S(1)}, u32[]{:S(2)}, u32[]{:S(2)}) %collective-permute-start.6) | collective-permute-done | bytes 1048608 | tf_op jit(solution)/shard_map/ppermute | solution.py:16
  471.8 23.8 %collective-permute-done.7 = f32[16,2,1,2,32,128]{5,4,3,2,1,0:T(8,128)S(1)} collective-permute-done((f32[16,2,1,2,32,128]{5,4,3,2,1,0:T(8,128)S(1)}, f32[16,2,1,2,32,128]{5,4,3,2,1,0:T(8,128)S(1)}, u32[]{:S(2)}, u32[]{:S(2)}) %collective-permute-start.7) | collective-permute-done | bytes 1048608 | tf_op jit(solution)/shard_map/ppermute | solution.py:16
  496.8 21.0 %collective-permute-done.11 = f32[16,1,1,4,32,128]{5,4,3,2,0,1:T(8,128)S(1)} collective-permute-done((f32[16,1,1,4,32,128]{5,4,3,2,0,1:T(8,128)S(1)}, f32[16,1,1,4,32,128]{5,4,3,2,0,1:T(8,128)S(1)}, u32[]{:S(2)}, u32[]{:S(2)}) %collective-permute-start.11) | collective-permute-done | bytes 1048608 | tf_op jit(solution)/shard_map/ppermute | solution.py:16
  519.3 18.3 %collective-permute-done.8 = f32[16,1,1,4,32,128]{5,4,3,2,0,1:T(8,128)S(1)} collective-permute-done((f32[16,1,1,4,32,128]{5,4,3,2,0,1:T(8,128)S(1)}, f32[16,1,1,4,32,128]{5,4,3,2,0,1:T(8,128)S(1)}, u32[]{:S(2)}, u32[]{:S(2)}) %collective-permute-start.8) | collective-permute-done | bytes 1048608 | tf_op jit(solution)/shard_map/ppermute | solution.py:16
  (128 shorter events, 94.0 us)
Async XLA Ops:
  0.6 3.7 copy-start
  4.3 3.3 copy-start.3
  7.6 3.3 copy-start.10
  7.6 4.0 copy-start.11
  12.3 4.3 copy-start.8
  16.6 30.2 %copy-start.4 = (f32[4096,128]{0,1:T(8,128)}, f32[4096,128]{0,1:T(8,128)S(1)}, u32[]{:S(2)}) copy-start(f32[4096,128]{0,1:T(8,128)S(1)} %fusion.1) | copy-start | bytes 6291460
  52.1 11.8 %copy-start.5 = (f32[4096,128]{0,1:T(8,128)S(1)}, f32[4096,128]{0,1:T(8,128)}, u32[]{:S(2)}) copy-start(f32[4096,128]{0,1:T(8,128)} %copy-done.4) | copy-start | bytes 6291460
  52.1 62.4 %all-to-all-start = ((f32[1,4,1024,128]{3,1,0,2:T(4,128)}), f32[1,4,1024,128]{3,1,0,2:T(4,128)}, u32[]{:S(2)}, u32[]{:S(2)}) async-start(f32[1,4,1024,128]{3,1,0,2:T(4,128)} %copy.132), calls=%async_computation | async-start | bytes 4194304 | tf_op jit(solution)/shard_map/all_to_all | solution.py:159
  114.5 10.3 %copy-start.9 = (f32[3,2,128,128]{3,2,1,0:T(8,128)S(1)}, f32[3,2,128,128]{3,2,1,0:T(8,128)}, u32[]{:S(2)}) copy-start(f32[3,2,128,128]{3,2,1,0:T(8,128)} %param.8) | copy-start | bytes 1179652
  114.5 58.1 %all-to-all-start.1 = ((f32[32,1,4,32,128]{4,3,2,1,0:T(8,128)}), f32[32,1,4,32,128]{4,3,2,1,0:T(8,128)S(1)}, u32[]{:S(2)}, u32[]{:S(2)}) async-start(f32[32,1,4,32,128]{4,3,2,1,0:T(8,128)} %constant_dynamic-update-slice_fusion), calls=%async_computation.1 | async-start | bytes 4194304 | tf_op jit(solution)/shard_map/all_to_all | solution.py:161
  172.6 3.0 copy-start.2
  180.4 51.7 %all-to-all-start.3 = ((f32[32,4,32,128]{3,2,1,0:T(8,128)}), f32[32,4,32,128]{3,2,1,0:T(8,128)}, u32[]{:S(2)}, u32[]{:S(2)}) async-start(f32[32,4,32,128]{3,2,1,0:T(8,128)} %bitcast.354), calls=%async_computation.3 | async-start | bytes 4194304 | tf_op jit(solution)/shard_map/all_to_all | solution.py:169
  232.1 58.3 %all-to-all-start.2 = ((f32[32,4,32,128]{3,2,1,0:T(8,128)}), f32[32,4,32,128]{3,2,1,0:T(8,128)}, u32[]{:S(2)}, u32[]{:S(2)}) async-start(f32[32,4,32,128]{3,2,1,0:T(8,128)} %bitcast.113), calls=%async_computation.2 | async-start | bytes 4194304 | tf_op jit(solution)/shard_map/all_to_all | solution.py:168
  246.3 67.5 %collective-permute-start.3 = (f32[16,4,1,1,32,128]{5,4,2,1,0,3:T(8,128)}, f32[16,4,1,1,32,128]{5,4,2,1,0,3:T(8,128)}, u32[]{:S(2)}, u32[]{:S(2)}) collective-permute-start(f32[16,4,1,1,32,128]{5,4,2,1,0,3:T(8,128)} %get-tuple-element.19), channel_id=1, source_target_pairs={{0,1},{1,0},{2,3},{3,2},{4,5},{5,4},{6,7},{7,6},{8,9},{9,8},{10,11... | collective-permute-start | bytes 3145736 | tf_op jit(solution)/shard_map/ppermute | solution.py:16
  293.4 42.9 %collective-permute-start = (f32[16,4,1,1,32,128]{5,4,2,1,0,3:T(8,128)}, f32[16,4,1,1,32,128]{5,4,2,1,0,3:T(8,128)}, u32[]{:S(2)}, u32[]{:S(2)}) collective-permute-start(f32[16,4,1,1,32,128]{5,4,2,1,0,3:T(8,128)} %get-tuple-element.25), channel_id=1, source_target_pairs={{0,1},{1,0},{2,3},{3,2},{4,5},{5,4},{6,7},{7,6},{8,9},{9,8},{10,11... | collective-permute-start | bytes 3145736 | tf_op jit(solution)/shard_map/ppermute | solution.py:16
  318.3 26.3 %collective-permute-start.4 = (f32[16,2,1,2,32,128]{5,4,3,2,1,0:T(8,128)}, f32[16,2,1,2,32,128]{5,4,3,2,1,0:T(8,128)}, u32[]{:S(2)}, u32[]{:S(2)}) collective-permute-start(f32[16,2,1,2,32,128]{5,4,3,2,1,0:T(8,128)} %get-tuple-element.17), channel_id=1, source_target_pairs={{0,2},{2,0},{1,3},{3,1},{4,6},{6,4},{5,7},{7,5},{8,10},{10,8},{9,1... | collective-permute-start | bytes 3145736 | tf_op jit(solution)/shard_map/ppermute | solution.py:16
  339.4 27.7 %collective-permute-start.1 = (f32[16,2,1,2,32,128]{5,4,3,2,1,0:T(8,128)}, f32[16,2,1,2,32,128]{5,4,3,2,1,0:T(8,128)}, u32[]{:S(2)}, u32[]{:S(2)}) collective-permute-start(f32[16,2,1,2,32,128]{5,4,3,2,1,0:T(8,128)} %get-tuple-element.23), channel_id=1, source_target_pairs={{0,2},{2,0},{1,3},{3,1},{4,6},{6,4},{5,7},{7,5},{8,10},{10,8},{9,1... | collective-permute-start | bytes 3145736 | tf_op jit(solution)/shard_map/ppermute | solution.py:16
  349.1 43.0 %collective-permute-start.5 = (f32[16,1,1,4,32,128]{5,4,3,2,0,1:T(8,128)}, f32[16,1,1,4,32,128]{5,4,3,2,0,1:T(8,128)}, u32[]{:S(2)}, u32[]{:S(2)}) collective-permute-start(f32[16,1,1,4,32,128]{5,4,3,2,0,1:T(8,128)} %get-tuple-element.15), channel_id=1, source_target_pairs={{0,4},{4,0},{1,5},{5,1},{2,6},{6,2},{3,7},{7,3},{8,12},{12,8},{9,1... | collective-permute-start | bytes 3145736 | tf_op jit(solution)/shard_map/ppermute | solution.py:16
  370.7 42.8 %collective-permute-start.2 = (f32[16,1,1,4,32,128]{5,4,3,2,0,1:T(8,128)}, f32[16,1,1,4,32,128]{5,4,3,2,0,1:T(8,128)}, u32[]{:S(2)}, u32[]{:S(2)}) collective-permute-start(f32[16,1,1,4,32,128]{5,4,3,2,0,1:T(8,128)} %get-tuple-element.21), channel_id=1, source_target_pairs={{0,4},{4,0},{1,5},{5,1},{2,6},{6,2},{3,7},{7,3},{8,12},{12,8},{9,1... | collective-permute-start | bytes 3145736 | tf_op jit(solution)/shard_map/ppermute | solution.py:16
  374.8 17.3 %copy-start.6 = (f32[16,1,1,4,32,128]{5,4,3,2,0,1:T(8,128)S(1)}, f32[16,1,1,4,32,128]{5,4,3,2,0,1:T(8,128)}, u32[]{:S(2)}) copy-start(f32[16,1,1,4,32,128]{5,4,3,2,0,1:T(8,128)} %get-tuple-element.14) | copy-start | bytes 3145732
  394.0 19.6 %copy-start.7 = (f32[16,1,1,4,32,128]{5,4,3,2,0,1:T(8,128)S(1)}, f32[16,1,1,4,32,128]{5,4,3,2,0,1:T(8,128)}, u32[]{:S(2)}) copy-start(f32[16,1,1,4,32,128]{5,4,3,2,0,1:T(8,128)} %get-tuple-element.20) | copy-start | bytes 3145732
  422.3 26.1 %collective-permute-start.9 = (f32[16,4,1,1,32,128]{5,4,2,1,0,3:T(8,128)S(1)}, f32[16,4,1,1,32,128]{5,4,2,1,0,3:T(8,128)S(1)}, u32[]{:S(2)}, u32[]{:S(2)}) collective-permute-start(f32[16,4,1,1,32,128]{5,4,2,1,0,3:T(8,128)S(1)} %get-tuple-element.7), channel_id=1, source_target_pairs={{0,1},{1,0},{2,3},{3,2},{4,5},{5,4},{6,7},{7,6},{8,9},{9,8},{10,11... | collective-permute-start | bytes 3145736 | tf_op jit(solution)/shard_map/ppermute | solution.py:16
  426.0 43.1 %collective-permute-start.6 = (f32[16,4,1,1,32,128]{5,4,2,1,0,3:T(8,128)S(1)}, f32[16,4,1,1,32,128]{5,4,2,1,0,3:T(8,128)S(1)}, u32[]{:S(2)}, u32[]{:S(2)}) collective-permute-start(f32[16,4,1,1,32,128]{5,4,2,1,0,3:T(8,128)S(1)} %get-tuple-element.13), channel_id=1, source_target_pairs={{0,1},{1,0},{2,3},{3,2},{4,5},{5,4},{6,7},{7,6},{8,9},{9,8},{10,11... | collective-permute-start | bytes 3145736 | tf_op jit(solution)/shard_map/ppermute | solution.py:16
  448.8 21.6 %collective-permute-start.10 = (f32[16,2,1,2,32,128]{5,4,3,2,1,0:T(8,128)S(1)}, f32[16,2,1,2,32,128]{5,4,3,2,1,0:T(8,128)S(1)}, u32[]{:S(2)}, u32[]{:S(2)}) collective-permute-start(f32[16,2,1,2,32,128]{5,4,3,2,1,0:T(8,128)S(1)} %get-tuple-element.5), channel_id=1, source_target_pairs={{0,2},{2,0},{1,3},{3,1},{4,6},{6,4},{5,7},{7,5},{8,10},{10,8},{9,1... | collective-permute-start | bytes 3145736 | tf_op jit(solution)/shard_map/ppermute | solution.py:16
  469.5 26.1 %collective-permute-start.7 = (f32[16,2,1,2,32,128]{5,4,3,2,1,0:T(8,128)S(1)}, f32[16,2,1,2,32,128]{5,4,3,2,1,0:T(8,128)S(1)}, u32[]{:S(2)}, u32[]{:S(2)}) collective-permute-start(f32[16,2,1,2,32,128]{5,4,3,2,1,0:T(8,128)S(1)} %get-tuple-element.11), channel_id=1, source_target_pairs={{0,2},{2,0},{1,3},{3,1},{4,6},{6,4},{5,7},{7,5},{8,10},{10,8},{9,1... | collective-permute-start | bytes 3145736 | tf_op jit(solution)/shard_map/ppermute | solution.py:16
  470.9 46.8 %collective-permute-start.11 = (f32[16,1,1,4,32,128]{5,4,3,2,0,1:T(8,128)S(1)}, f32[16,1,1,4,32,128]{5,4,3,2,0,1:T(8,128)S(1)}, u32[]{:S(2)}, u32[]{:S(2)}) collective-permute-start(f32[16,1,1,4,32,128]{5,4,3,2,0,1:T(8,128)S(1)} %get-tuple-element.3), channel_id=1, source_target_pairs={{0,4},{4,0},{1,5},{5,1},{2,6},{6,2},{3,7},{7,3},{8,12},{12,8},{9,1... | collective-permute-start | bytes 3145736 | tf_op jit(solution)/shard_map/ppermute | solution.py:16
  496.0 41.5 %collective-permute-start.8 = (f32[16,1,1,4,32,128]{5,4,3,2,0,1:T(8,128)S(1)}, f32[16,1,1,4,32,128]{5,4,3,2,0,1:T(8,128)S(1)}, u32[]{:S(2)}, u32[]{:S(2)}) collective-permute-start(f32[16,1,1,4,32,128]{5,4,3,2,0,1:T(8,128)S(1)} %get-tuple-element.9), channel_id=1, source_target_pairs={{0,4},{4,0},{1,5},{5,1},{2,6},{6,2},{3,7},{7,3},{8,12},{12,8},{9,1... | collective-permute-start | bytes 3145736 | tf_op jit(solution)/shard_map/ppermute | solution.py:16
  537.5 2.3 copy-start.1
